TPU v7x, 32 devices: a whole 2x2x4 slice. The times are simulated.
32 devices in a mesh: dp: 4 (over y, core), ctx: 4 (over z), tsp: 2 (over x).
Axes of the slice: x: 2, y: 2, z: 4, core: 2. Of those that a mesh axis runs over, the one named last changes fastest.
Arguments:
- grad_out: bfloat16 [4, 1024, 8192], P('dp', 'ctx', 'tsp'), may hold values from -6 to 6
- attn_out: bfloat16 [4, 1024, 4096], P('dp', None, 'ctx'), may hold values from -6 to 6
- out_weight: bfloat16 [4096, 8192], P('ctx', 'tsp'), may hold values from -0.0625 to 0.0625
- query: bfloat16 [4, 1024, 4096], P('dp', 'tsp', 'ctx'), may hold values from -128 to 128
- keys: bfloat16 [4, 1024, 512], P('dp'), may hold values from -128 to 128
- values: bfloat16 [4, 1024, 512], P('dp'), may hold values from -6 to 6
- segment_ids: int32 [4, 1024], P('dp'), may hold values from 0 to 7, never falling along the last dimension, each value on 1 to 256 neighbouring positions
- tile_live: int32 [4, 8, 8], P('dp'), may hold values 0 or 1
Outputs:
- grad_query: bfloat16 [4, 1024, 4096], P('dp', 'tsp', 'ctx')
- grad_keys: bfloat16 [4, 1024, 512], P('dp', ('ctx', 'tsp'))
- grad_values: bfloat16 [4, 1024, 512], P('dp', ('ctx', 'tsp'))
- grad_weight: float32 [4096, 8192], P('ctx', 'tsp')
Inputs may be any that keep to these rules, and one draw needn't show every extreme that they name: `segment_ids`: segment numbers never fall along a row and segment 0 is the source document; each segment has 1 to 256 tokens, one exactly that many.
All inputs are finite; a program needn't handle non-finite values. No bound on the sum of `tile_live` on one device may be relied on, other than what follows from the above.
Results may differ from a plain program's by a relative error of at most 0.0058.
Values may be sent and summed in bfloat16 or wider, within the bound.
A program may use at most 128 MiB of HBM per device.

v0:
```python
import math
import jax
import jax.numpy as jnp
from jax import lax
from jax.sharding import PartitionSpec as P

HEADS = 32
KV_HEADS = 4
HEAD_DIM = 128
TILE = 128


def merge_group(tensor_in):
    row_count = tensor_in.shape[0]
    folded = tensor_in.reshape(row_count, KV_HEADS, HEADS // KV_HEADS, HEAD_DIM).sum(axis=2)
    return folded.reshape(row_count, KV_HEADS * HEAD_DIM)


def per_device(grad_out, attn_out, out_weight, query, keys, values, segment_ids, tile_live):
    score_scale = 1.0 / math.sqrt(HEAD_DIM)
    out_all = attn_out[0]
    seq_len = out_all.shape[0]
    feat_width = out_all.shape[1]
    dy_block = lax.all_gather(grad_out, "ctx", axis=1, tiled=True)[0]
    proj_rows = lax.dot_general(
        dy_block, out_weight, (((1,), (1,)), ((), ())), preferred_element_type=jnp.float32
    )
    grad_part = proj_rows
    weight_part = lax.dot_general(
        out_all, dy_block, (((0,), (0,)), ((), ())), preferred_element_type=jnp.float32
    )
    grad_part, weight_part = (grad_part, weight_part)
    grad_weight = lax.psum(weight_part, "dp")
    out_grad = lax.psum_scatter(grad_part, "tsp", scatter_dimension=0, tiled=True).astype(
        jnp.bfloat16
    )
    quarter = out_grad.shape[0]
    row_start = lax.axis_index("tsp") * quarter
    heads_dev = feat_width // HEAD_DIM
    group_size = HEADS // KV_HEADS
    head_ids = lax.axis_index("ctx") * heads_dev + jnp.arange(heads_dev, dtype=jnp.int32)
    kv_ids = head_ids // group_size
    query_pos = row_start + jnp.arange(quarter, dtype=jnp.int32)
    key_pos = jnp.arange(seq_len, dtype=jnp.int32)
    tile_count = seq_len // TILE
    tile_rows = lax.dynamic_slice_in_dim(tile_live[0], row_start // TILE, quarter // TILE, 0)
    tile_mask = (
        jnp.broadcast_to(
            tile_rows[:, None, :, None], (quarter // TILE, TILE, tile_count, TILE)
        ).reshape(quarter, seq_len)
        == 1
    )
    same_tile = query_pos[:, None] // TILE == key_pos[None, :] // TILE
    segments = segment_ids[0]
    query_seg = lax.dynamic_slice_in_dim(segments, row_start, quarter, 0)
    same_doc = (segments[None, :] == query_seg[:, None]) | (segments[None, :] == 0)
    allowed = (tile_mask | same_tile) & same_doc & (key_pos[None, :] <= query_pos[:, None])

    def split_heads(tensor_in):
        return tensor_in.reshape(tensor_in.shape[0], heads_dev, HEAD_DIM).transpose(1, 0, 2)

    query_heads = split_heads(query[0])
    grad_heads = split_heads(out_grad)
    output_heads = split_heads(lax.dynamic_slice_in_dim(out_all, row_start, quarter, 0))
    key_table = keys[0].reshape(seq_len, KV_HEADS, HEAD_DIM)
    value_table = values[0].reshape(seq_len, KV_HEADS, HEAD_DIM)

    def one_head(head_items):
        query_head, grad_head, output_head, kv_index = head_items
        key_head = lax.dynamic_index_in_dim(key_table, kv_index, 1, keepdims=False)
        value_head = lax.dynamic_index_in_dim(value_table, kv_index, 1, keepdims=False)
        scores = (
            lax.dot_general(
                query_head, key_head, (((1,), (1,)), ((), ())), preferred_element_type=jnp.float32
            )
            * score_scale
        )
        scores = jnp.where(allowed, scores, -jnp.inf)
        row_max = jnp.max(scores, axis=1, keepdims=True)
        lse = row_max + jnp.log(jnp.sum(jnp.exp(scores - row_max), axis=1, keepdims=True))
        probs_f = jnp.where(allowed, jnp.exp(scores - lse), 0.0)
        probs = probs_f.astype(jnp.bfloat16)
        value_term = lax.dot_general(
            probs, grad_head, (((0,), (0,)), ((), ())), preferred_element_type=jnp.float32
        )
        dprobs = lax.dot_general(
            grad_head, value_head, (((1,), (1,)), ((), ())), preferred_element_type=jnp.float32
        )
        delta = jnp.sum(
            grad_head.astype(jnp.float32) * output_head.astype(jnp.float32), axis=1, keepdims=True
        )
        dscores = (probs_f * (dprobs - delta)).astype(jnp.bfloat16)
        query_grad = (
            jnp.dot(dscores, key_head, preferred_element_type=jnp.float32) * score_scale
        ).astype(jnp.bfloat16)
        key_term = (
            lax.dot_general(
                dscores, query_head, (((0,), (0,)), ((), ())), preferred_element_type=jnp.float32
            )
            * score_scale
        )
        return (query_grad, key_term, value_term)

    query_grads, key_terms, value_terms = lax.map(
        one_head, (query_heads, grad_heads, output_heads, kv_ids)
    )
    grad_query = query_grads.transpose(1, 0, 2).reshape(quarter, feat_width)
    key_cols = key_terms.transpose(1, 0, 2).reshape(seq_len, feat_width)
    value_cols = value_terms.transpose(1, 0, 2).reshape(seq_len, feat_width)
    key_recv, value_recv = (
        lax.all_to_all(key_cols, "ctx", split_axis=0, concat_axis=1, tiled=True),
        lax.all_to_all(value_cols, "ctx", split_axis=0, concat_axis=1, tiled=True),
    )
    key_part, value_part = (
        lax.psum_scatter(merge_group(key_recv), "tsp", scatter_dimension=0, tiled=True),
        lax.psum_scatter(merge_group(value_recv), "tsp", scatter_dimension=0, tiled=True),
    )
    grad_keys = key_part.astype(jnp.bfloat16)[None]
    grad_values = value_part.astype(jnp.bfloat16)[None]
    return (grad_query[None], grad_keys, grad_values, grad_weight)


def solution(mesh):
    placed = (
        P("dp", "ctx", "tsp"),
        P("dp", None, "ctx"),
        P("ctx", "tsp"),
        P("dp", "tsp", "ctx"),
        P("dp", None, None),
        P("dp", None, None),
        P("dp", None),
        P("dp", None, None),
    )
    return jax.shard_map(
        per_device,
        mesh=mesh,
        in_specs=placed,
        out_specs=(
            P("dp", "tsp", "ctx"),
            P("dp", ("ctx", "tsp"), None),
            P("dp", ("ctx", "tsp"), None),
            P("ctx", "tsp"),
        ),
        check_vma=False,
    )
```

profile of v0, /device:TPU:0, one launch (start us, length us, event | category | flops | bytes accessed | tf_op | source)
XLA Modules:
  0.0 900.4 jit_solution(15618256980744114519)
XLA Ops:
  8.0 154.0 %all-gather.2.cloned.1.call-done = bf16[1,1024,4096]{2,1,0:T(8,128)(2,1)} async-done(((bf16[1,256,4096]{2,1,0:T(8,128)(2,1)}), bf16[1,1024,4096]{2,1,0:T(8,128)(2,1)}) %all-gather.2.cloned.1.call-update) | async-done | bytes 8388624 | tf_op jit(solution)/shard_map/all_gather | solution.py:24
  161.9 15.1 %fusion.38 = f32[1024,1024]{1,0:T(8,128)} fusion(bf16[1024,4096]{1,0:T(8,128)(2,1)} %param.12, bf16[1,1024,4096]{2,1,0:T(8,128)(2,1)} %all-gather.2.cloned.1.call-done), kind=kOutput, calls=%fused_computation.47 | convolution fusion | flops 8589934592 | bytes 20971520 | tf_op jit(solution)/shard_map/dot_general | solution.py:25
  177.2 1.3 copy.66
  178.5 2.4 copy.46
  182.3 2.3 copy.49
  184.7 45.1 %reduce-scatter.4.cloned.1.call-done = f32[512,1024]{1,0:T(8,128)} async-done(((f32[1024,1024]{1,0:T(8,128)}), f32[512,1024]{1,0:T(8,128)}) %reduce-scatter.4.cloned.1.call-update) | async-done | bytes 2097168 | tf_op jit(solution)/shard_map/reduce_scatter | solution.py:34
  229.7 1.7 bitcast_bitcast_fusion
  231.5 129.6 %while.15 = (s32[]{:T(128)}, bf16[8,512,128]{2,1,0:T(8,128)(2,1)}, f32[8,1024,128]{2,1,0:T(8,128)}, f32[8,1024,128]{2,1,0:T(8,128)}, bf16[8,512,128]{1,2,0:T(8,1...) while((s32[]{:T(128)}, bf16[8,512,128]{2,1,0:T(8,128)(2,1)}, ...), condition=%wide.region_5.6_spmd.clone, body=%wide.region_1.5_spmd.clone.sunk | while | flops 689437696 | bytes 16977196 | solution.py:104
  235.4 2.4 fusion.73
  238.3 2.7 multiply_convert_fusion.2
  241.1 2.1 fusion.75
  243.1 2.4 fusion.77
  245.5 2.2 fusion.76
  251.6 2.4 fusion.73
  254.5 2.7 multiply_convert_fusion.2
  257.3 2.1 fusion.75
  259.3 2.4 fusion.77
  261.8 2.2 fusion.76
  267.9 2.4 fusion.73
  270.8 2.7 multiply_convert_fusion.2
  273.5 2.1 fusion.75
  275.6 2.4 fusion.77
  278.0 2.2 fusion.76
  284.1 2.4 fusion.73
  287.0 2.7 multiply_convert_fusion.2
  289.7 2.1 fusion.75
  291.8 2.4 fusion.77
  294.1 2.2 fusion.76
  300.3 2.4 fusion.73
  303.2 2.7 multiply_convert_fusion.2
  305.9 2.1 fusion.75
  308.0 2.4 fusion.77
  310.4 2.2 fusion.76
  316.5 2.4 fusion.73
  319.4 2.7 multiply_convert_fusion.2
  322.1 2.1 fusion.75
  324.2 2.4 fusion.77
  326.5 2.2 fusion.76
  332.7 2.4 fusion.73
  335.6 2.7 multiply_convert_fusion.2
  338.3 2.1 fusion.75
  340.4 2.4 fusion.77
  342.7 2.2 fusion.76
  348.9 2.4 fusion.73
  351.7 2.7 multiply_convert_fusion.2
  354.5 2.1 fusion.75
  356.5 2.4 fusion.77
  358.9 2.2 fusion.76
  361.1 6.6 copy.58
  367.7 4.9 all_to_all.27
  372.6 4.9 all-to-all-start.1
  377.5 6.5 copy.56
  384.0 4.9 all_to_all.24
  388.9 81.9 %all-to-all-done.1 = f32[4,256,1024]{2,1,0:T(8,128)} async-done(((f32[4,256,1024]{2,1,0:T(8,128)}), f32[4,256,1024]{2,1,0:T(8,128)}, u32[]{:S(2)}, u32[]{:S(2)}) %all-to-all-start.1) | async-done | bytes 4194336 | tf_op jit(solution)/shard_map/all_to_all | solution.py:112
  470.8 4.9 all-to-all-start
  475.8 5.1 copy.70
  480.9 3.2 reduce_sum.37
  485.2 83.3 %all-to-all-done = f32[4,256,1024]{2,1,0:T(8,128)} async-done(((f32[4,256,1024]{2,1,0:T(8,128)}), f32[4,256,1024]{2,1,0:T(8,128)}, u32[]{:S(2)}, u32[]{:S(2)}) %all-to-all-start) | async-done | bytes 4194336 | tf_op jit(solution)/shard_map/all_to_all | solution.py:111
  568.5 5.2 copy.69
  573.7 3.2 reduce_sum.36
  578.0 15.0 %fusion.36 = f32[1024,4096]{1,0:T(8,128)} fusion(bf16[1,1024,4096]{2,1,0:T(8,128)(2,1)} %all-gather.2.cloned.1.call-done, bf16[1,1024,1024]{2,1,0:T(8,128)(2,1)S(1)} %copy-done), kind=kOutput, calls=%fused_computation.45 | convolution fusion | flops 8589934592 | bytes 27262976 | tf_op jit(solution)/shard_map/dot_general | solution.py:29
  593.0 1.9 copy.55
  599.7 282.5 %all-reduce.2.cloned.1.call-done = f32[1024,4096]{1,0:T(8,128)} async-done(((f32[1024,4096]{1,0:T(8,128)}), f32[1024,4096]{1,0:T(8,128)}) %all-reduce.2.cloned.1.call-update) | async-done | bytes 16777232 | tf_op jit(solution)/shard_map/psum | solution.py:33
  882.2 11.7 %copy.104 = f32[1024,4096]{1,0:T(8,128)} copy(f32[1024,4096]{1,0:T(8,128)} %all-reduce.2.cloned.1.call-done) | data formatting | bytes 33554432
  (94 shorter events, 29.3 us)
Async XLA Ops:
  7.2 169.9 %copy-start = (bf16[1,1024,1024]{2,1,0:T(8,128)(2,1)S(1)}, bf16[1,1024,1024]{2,1,0:T(8,128)(2,1)}, u32[]{:S(2)}) copy-start(bf16[1,1024,1024]{2,1,0:T(8,128)(2,1)} %param.11) | copy-start | bytes 6291460
  7.2 154.7 %all-gather.2.cloned.1.call-start = ((), (), s32[]{:S(2)}) async-start(), calls=%async_computation.5 | async-start | bytes 10485760 | tf_op jit(solution)/shard_map/all_gather | solution.py:24
  7.9 221.8 %reduce-scatter.4.cloned.1.call-start = ((), (), s32[]{:S(2)}) async-start(), calls=%async_computation.6 | async-start | bytes 6291456 | tf_op jit(solution)/shard_map/reduce_scatter | solution.py:34
  178.5 2.4 copy-start.1
  180.9 3.6 copy-start.3
  180.9 3.7 copy-start.2
  372.6 98.3 %all-to-all-start.1 = ((f32[4,256,1024]{2,1,0:T(8,128)}), f32[4,256,1024]{2,1,0:T(8,128)}, u32[]{:S(2)}, u32[]{:S(2)}) async-start(f32[4,256,1024]{2,1,0:T(8,128)} %all_to_all.27), calls=%async_computation.3 | async-start | bytes 8388608 | tf_op jit(solution)/shard_map/all_to_all | solution.py:112
  470.8 97.7 %all-to-all-start = ((f32[4,256,1024]{2,1,0:T(8,128)}), f32[4,256,1024]{2,1,0:T(8,128)}, u32[]{:S(2)}, u32[]{:S(2)}) async-start(f32[4,256,1024]{2,1,0:T(8,128)} %all_to_all.24), calls=%async_computation.1 | async-start | bytes 8388608 | tf_op jit(solution)/shard_map/all_to_all | solution.py:111
  475.8 120.4 %reduce-scatter.8.cloned.1.call-start = ((), (), s32[]{:S(2)}) async-start(), calls=%async_computation.8 | async-start | bytes 786432 | tf_op jit(solution)/shard_map/reduce_scatter | solution.py:116
  485.1 112.8 %reduce-scatter.6.cloned.1.call-start = ((), (), s32[]{:S(2)}) async-start(), calls=%async_computation.7 | async-start | bytes 786432 | tf_op jit(solution)/shard_map/reduce_scatter | solution.py:115
  578.0 304.2 %all-reduce.2.cloned.1.call-start = ((), (), s32[]{:S(2)}) async-start(), calls=%async_computation.9 | async-start | bytes 33554432 | tf_op jit(solution)/shard_map/psum | solution.py:33
Sparse Core Ops, SparseCore 0:
  9.6 152.3 all-gather.1
  177.1 52.5 reduce-scatter.3
  485.3 15.0 reduce-scatter.7
  578.1 12.7 reduce-scatter.5
  593.8 288.3 all-reduce.1
where the time goes:
time: 902 us; the launch traced here: 900 us
  waiting for transfers between devices  648 us (72%)
  matrix products  124 us (14%)
  local copies, waits for them, and re-layouts  73.7 us (8%)
  loops' own time  15.8 us (2%)
  other arithmetic  15.5 us (2%)
  between operations  13.9 us (2%)
  starting transfers between devices  10.1 us (1%)
    psum x1, waiting for transfers between devices, per_device(): grad_weight = lax.psum(weight_part, 'dp')  282 us
    all_gather x1, waiting for transfers between devices, per_device(): dy_block = lax.all_gather(grad_out, 'ctx', axis=1, tiled=True)[0]  154 us
    all_to_all x1, waiting for transfers between devices, per_device(): lax.all_to_all(key_cols, 'ctx', split_axis=0, concat_axis=1, tiled=True)  83.3 us
    all_to_all x1, waiting for transfers between devices, per_device(): lax.all_to_all(value_cols, 'ctx', split_axis=0, concat_axis=1, tiled=True)  81.9 us
    reduce_scatter x1, waiting for transfers between devices, per_device(): lax.psum_scatter(grad_part, 'tsp', scatter_dimension=0, tiled=True)  45.1 us
    unnamed x17, local copies, waits for them, and re-layouts  31 us
    dot_general x8, matrix products, one_head(): lax.dot_general(grad_head, value_head, (((1,), (1,)), ((), ())), preferre...  21.9 us
    dot_general x8, matrix products, one_head(): lax.dot_general(probs, grad_head, (((0,), (0,)), ((), ())), preferred_ele...  19.1 us
  transfers between devices with their start and end apart: 7, of which 5 were waited for; matrix products, arithmetic and copies ran while one was open for 6% of the time, Pallas kernels for 0%

commit v1 on v0

--- a/solution.py
+++ b/solution.py
@@ -8,6 +8,22 @@
 KV_HEADS = 4
 HEAD_DIM = 128
 TILE = 128
+
+
+def collect(x, axis, dim):
+    ways, here, step = (lax.axis_size(axis), lax.axis_index(axis), x.shape[dim])
+    dims = [n * ways if d == dim else n for d, n in enumerate(x.shape)]
+    full = lax.dynamic_update_slice_in_dim(jnp.zeros(dims, x.dtype), x, here * step, axis=dim)
+    going_up = going_down = x
+    for far in range(1, ways // 2 + 1):
+        going_up = lax.ppermute(going_up, axis, [(d, (d + 1) % ways) for d in range(ways)])
+        full = lax.dynamic_update_slice_in_dim(full, going_up, (here - far) % ways * step, axis=dim)
+        if 2 * far < ways:
+            going_down = lax.ppermute(going_down, axis, [(d, (d - 1) % ways) for d in range(ways)])
+            full = lax.dynamic_update_slice_in_dim(
+                full, going_down, (here + far) % ways * step, axis=dim
+            )
+    return full
 
 
 def merge_group(tensor_in):
@@ -21,7 +37,7 @@
     out_all = attn_out[0]
     seq_len = out_all.shape[0]
     feat_width = out_all.shape[1]
-    dy_block = lax.all_gather(grad_out, "ctx", axis=1, tiled=True)[0]
+    dy_block = collect(grad_out, "ctx", 1)[0]
     proj_rows = lax.dot_general(
         dy_block, out_weight, (((1,), (1,)), ((), ())), preferred_element_type=jnp.float32
     )

time: 902 us -> 740 us (0.82)
  waiting for transfers between devices: 648 us -> 419 us
  other arithmetic: 15.5 us -> 37.1 us
  local copies, waits for them, and re-layouts: 73.7 us -> 95.3 us
  matrix products: 124 us -> 139 us
    psum x1, waiting for transfers between devices: 282 us -> 99.8 us  [per_device(): grad_weight = lax.psum(weight_part, 'dp')]
    all_gather x1 -> x0, waiting for transfers between devices: 154 us -> none  [per_device(): dy_block = lax.all_gather(grad_out, 'ctx', axis=1, tiled=True)[0]]
    ppermute x0 -> x3, waiting for transfers between devices: none -> 124 us  [the longest x2 89 us: collect(): lax.ppermute(going_up, axis, [(d, (d + 1) % ways) for d in range(ways)])]
    all_to_all x1, waiting for transfers between devices: 83.3 us -> 66.5 us  [per_device(): lax.all_to_all(key_cols, 'ctx', split_axis=0, concat_axis=1, tiled=True)]
    reduce_sum x8, other arithmetic: 4.12 us -> 16.3 us  [one_head(): jnp.sum(jnp.exp(scores - row_max), axis=1, keepdims=True)]
    dynamic_update_slice x0 -> x4, local copies, waits for them, and re-layouts: none -> 10.9 us  [the longest x2 6.29 us: collect(): lax.dynamic_update_slice_in_dim(full, going_up, (here - far) % ways * ste...]
    dot_general x8, matrix products: 18.9 us -> 29.4 us  [one_head(): lax.dot_general(query_head, key_head, (((1,), (1,)), ((), ())), preferred...]
    unnamed x17 -> x21, local copies, waits for them, and re-layouts: 31 us -> 36.9 us
  transfers between devices with their start and end apart: 7 -> 9, of which waited for: 5 -> 7; matrix products, arithmetic and copies ran while one was open for 6% -> 11% of each run, Pallas kernels for 0% -> 0%
where the time goes in v1:
time: 740 us; the launch traced here: 738 us
  waiting for transfers between devices  419 us (57%)
  matrix products  139 us (19%)
  local copies, waits for them, and re-layouts  95.3 us (13%)
  other arithmetic  37.1 us (5%)
  loops' own time  15.9 us (2%)
  starting transfers between devices  15.4 us (2%)
  between operations  15.3 us (2%)
    psum x1, waiting for transfers between devices, per_device(): grad_weight = lax.psum(weight_part, 'dp')  99.8 us
    ppermute x2, waiting for transfers between devices, collect(): lax.ppermute(going_up, axis, [(d, (d + 1) % ways) for d in range(ways)])  89 us
    all_to_all x1, waiting for transfers between devices, per_device(): lax.all_to_all(value_cols, 'ctx', split_axis=0, concat_axis=1, tiled=True)  83 us
    all_to_all x1, waiting for transfers between devices, per_device(): lax.all_to_all(key_cols, 'ctx', split_axis=0, concat_axis=1, tiled=True)  66.5 us
    reduce_scatter x1, waiting for transfers between devices, per_device(): lax.psum_scatter(grad_part, 'tsp', scatter_dimension=0, tiled=True)  46.1 us
    unnamed x21, local copies, waits for them, and re-layouts  36.9 us
    ppermute x1, waiting for transfers between devices, collect(): lax.ppermute(going_down, axis, [(d, (d - 1) % ways) for d in range(ways)])  34.8 us
    dot_general x8, matrix products, one_head(): lax.dot_general(query_head, key_head, (((1,), (1,)), ((), ())), preferred...  29.4 us
  transfers between devices with their start and end apart: 9, of which 7 were waited for; matrix products, arithmetic and copies ran while one was open for 11% of the time, Pallas kernels for 0%

profile of v1, /device:TPU:0, one launch (start us, length us, event | category | flops | bytes accessed | tf_op | source)
XLA Modules:
  0.0 737.5 jit_solution(16312091321168364071)
XLA Ops:
  8.1 3.1 collective-permute-start
  11.2 2.1 collective-permute-start.1
  13.3 46.8 %collective-permute-done = bf16[1,256,4096]{2,1,0:T(8,128)(2,1)} collective-permute-done((bf16[1,256,4096]{2,1,0:T(8,128)(2,1)}, bf16[1,256,4096]{2,1,0:T(8,128)(2,1)}, u32[]{:S(2)}, u32[]{:S(2)}) %collective-permute-start) | collective-permute-done | bytes 2097184 | tf_op jit(solution)/shard_map/ppermute | solution.py:19
  60.0 4.3 squeeze.35
  65.8 3.2 bitcast_dynamic-update-slice_fusion.2
  69.0 34.8 %collective-permute-done.1 = bf16[1,256,4096]{2,1,0:T(8,128)(2,1)} collective-permute-done((bf16[1,256,4096]{2,1,0:T(8,128)(2,1)}, bf16[1,256,4096]{2,1,0:T(8,128)(2,1)}, u32[]{:S(2)}, u32[]{:S(2)}) %collective-permute-start.1) | collective-permute-done | bytes 2097184 | tf_op jit(solution)/shard_map/ppermute | solution.py:22
  103.7 3.1 bitcast_dynamic-update-slice_fusion.1
  106.9 42.2 %collective-permute-done.2 = bf16[1,256,4096]{2,1,0:T(8,128)(2,1)} collective-permute-done((bf16[1,256,4096]{2,1,0:T(8,128)(2,1)}, bf16[1,256,4096]{2,1,0:T(8,128)(2,1)}, u32[]{:S(2)}, u32[]{:S(2)}) %collective-permute-start.2) | collective-permute-done | bytes 2097184 | tf_op jit(solution)/shard_map/ppermute | solution.py:19
  149.1 3.1 bitcast_dynamic-update-slice_fusion
  152.2 15.1 %fusion.45 = f32[1024,1024]{1,0:T(8,128)} fusion(bf16[1024,4096]{1,0:T(8,128)(2,1)} %bitcast_dynamic-update-slice_fusion, bf16[1024,4096]{1,0:T(8,128)(2,1)} %param.12), kind=kOutput, calls=%fused_computation.81 | convolution fusion | flops 8589934592 | bytes 20971520 | tf_op jit(solution)/shard_map/dot_general | solution.py:41
  169.8 2.4 copy.51
  175.1 46.1 %reduce-scatter.4.cloned.1.call-done = f32[512,1024]{1,0:T(8,128)} async-done(((f32[1024,1024]{1,0:T(8,128)}), f32[512,1024]{1,0:T(8,128)}) %reduce-scatter.4.cloned.1.call-update) | async-done | bytes 2097168 | tf_op jit(solution)/shard_map/reduce_scatter | solution.py:50
  221.1 2.7 bitcast_bitcast_fusion
  223.8 165.9 %while.15 = (s32[]{:T(128)}, bf16[8,512,128]{2,1,0:T(8,128)(2,1)}, f32[8,1024,128]{2,1,0:T(8,128)}, f32[8,1024,128]{2,1,0:T(8,128)}, bf16[8,512,128]{1,2,0:T(8,1...) while((s32[]{:T(128)}, bf16[8,512,128]{2,1,0:T(8,128)(2,1)}, ...), condition=%wide.region_5.6_spmd.clone, body=%wide.region_1.5_spmd.clone.sunk | while | flops 689437696 | bytes 25365832 | solution.py:120
  226.6 3.7 fusion.72
  234.6 2.5 multiply_convert_fusion.2
  239.1 2.2 fusion.75
  241.3 3.2 fusion.76
  247.3 3.7 fusion.72
  255.3 2.5 multiply_convert_fusion.2
  259.9 2.2 fusion.75
  262.0 3.3 fusion.76
  268.0 3.7 fusion.72
  276.0 2.5 multiply_convert_fusion.2
  280.6 2.2 fusion.75
  282.8 3.3 fusion.76
  288.8 3.7 fusion.72
  296.8 2.5 multiply_convert_fusion.2
  299.3 2.1 fusion.74
  301.3 2.2 fusion.75
  303.5 3.3 fusion.76
  309.5 3.7 fusion.72
  317.5 2.5 multiply_convert_fusion.2
  322.1 2.2 fusion.75
  324.2 3.3 fusion.76
  330.2 3.7 fusion.72
  338.2 2.5 multiply_convert_fusion.2
  340.8 2.1 fusion.74
  342.8 2.2 fusion.75
  345.0 3.3 fusion.76
  351.0 3.7 fusion.72
  359.0 2.5 multiply_convert_fusion.2
  363.6 2.2 fusion.75
  365.7 3.2 fusion.76
  371.7 3.7 fusion.72
  379.7 2.5 multiply_convert_fusion.2
  382.2 2.1 fusion.74
  384.3 2.2 fusion.75
  386.4 3.3 fusion.76
  389.7 6.6 copy.60
  396.3 4.9 all_to_all.24
  401.2 4.9 all-to-all-start
  406.1 14.7 %convolution_bitcast_fusion.1 = f32[1024,4096]{0,1:T(8,128)} fusion(bf16[1024,4096]{1,0:T(8,128)(2,1)} %bitcast_dynamic-update-slice_fusion, bf16[1,1024,1024]{2,1,0:T(8,128)(2,1)S(1)} %copy-done), kind=kOutput, calls=%fused_computation.45 | convolution fusion | flops 8589934592 | bytes 27262976 | tf_op jit(solution)/shard_map/dot_general | solution.py:45
  420.9 7.0 copy.62
  427.9 4.9 all_to_all.27
  432.8 66.5 %all-to-all-done = f32[4,256,1024]{2,1,0:T(8,128)} async-done(((f32[4,256,1024]{2,1,0:T(8,128)}), f32[4,256,1024]{2,1,0:T(8,128)}, u32[]{:S(2)}, u32[]{:S(2)}) %all-to-all-start) | async-done | bytes 4194336 | tf_op jit(solution)/shard_map/all_to_all | solution.py:127
  499.3 4.9 all-to-all-start.1
  504.6 5.1 copy.74
  509.7 3.2 reduce_sum.36
  514.0 83.0 %all-to-all-done.1 = f32[4,256,1024]{2,1,0:T(8,128)} async-done(((f32[4,256,1024]{2,1,0:T(8,128)}), f32[4,256,1024]{2,1,0:T(8,128)}, u32[]{:S(2)}, u32[]{:S(2)}) %all-to-all-start.1) | async-done | bytes 4194336 | tf_op jit(solution)/shard_map/all_to_all | solution.py:128
  597.0 5.2 copy.75
  602.2 3.2 reduce_sum.37
  609.7 99.8 %all-reduce.2.cloned.1.call-done = f32[1024,4096]{0,1:T(8,128)} async-done(((f32[1024,4096]{0,1:T(8,128)}), f32[1024,4096]{0,1:T(8,128)}) %all-reduce.2.cloned.1.call-update) | async-done | bytes 16777232 | tf_op jit(solution)/shard_map/psum | solution.py:49
  709.5 17.4 %copy.66 = f32[1024,4096]{1,0:T(8,128)} copy(f32[1024,4096]{0,1:T(8,128)} %all-reduce.2.cloned.1.call-done) | data formatting | bytes 33554432
  (122 shorter events, 66.8 us)
Async XLA Ops:
  8.0 165.5 %copy-start = (bf16[1,1024,1024]{2,1,0:T(8,128)(2,1)S(1)}, bf16[1,1024,1024]{2,1,0:T(8,128)(2,1)}, u32[]{:S(2)}) copy-start(bf16[1,1024,1024]{2,1,0:T(8,128)(2,1)} %param.11) | copy-start | bytes 6291460
  8.0 213.1 %reduce-scatter.4.cloned.1.call-start = ((), (), s32[]{:S(2)}) async-start(), calls=%async_computation.5 | async-start | bytes 6291456 | tf_op jit(solution)/shard_map/reduce_scatter | solution.py:50
  8.1 52.0 %collective-permute-start = (bf16[1,256,4096]{2,1,0:T(8,128)(2,1)}, bf16[1,256,4096]{2,1,0:T(8,128)(2,1)}, u32[]{:S(2)}, u32[]{:S(2)}) collective-permute-start(bf16[1,256,4096]{2,1,0:T(8,128)(2,1)} %param.10), channel_id=1, source_target_pairs={{0,2},{2,4},{4,6},{6,0},{1,3},{3,5},{5,7},{7,1},{8,10},{10,12},{12... | collective-permute-start | bytes 6291464 | tf_op jit(solution)/shard_map/ppermute | solution.py:19
  11.2 92.6 %collective-permute-start.1 = (bf16[1,256,4096]{2,1,0:T(8,128)(2,1)}, bf16[1,256,4096]{2,1,0:T(8,128)(2,1)}, u32[]{:S(2)}, u32[]{:S(2)}) collective-permute-start(bf16[1,256,4096]{2,1,0:T(8,128)(2,1)} %param.10), channel_id=1, source_target_pairs={{0,6},{2,0},{4,2},{6,4},{1,7},{3,1},{5,3},{7,5},{8,14},{10,8},{12,... | collective-permute-start | bytes 6291464 | tf_op jit(solution)/shard_map/ppermute | solution.py:22
  13.3 51.1 %copy-start.2 = (bf16[1,256,4096]{2,1,0:T(8,128)(2,1)S(1)}, bf16[1,256,4096]{2,1,0:T(8,128)(2,1)}, u32[]{:S(2)}) copy-start(bf16[1,256,4096]{2,1,0:T(8,128)(2,1)} %param.10) | copy-start | bytes 6291460
  60.0 89.0 %collective-permute-start.2 = (bf16[1,256,4096]{2,1,0:T(8,128)(2,1)}, bf16[1,256,4096]{2,1,0:T(8,128)(2,1)}, u32[]{:S(2)}, u32[]{:S(2)}) collective-permute-start(bf16[1,256,4096]{2,1,0:T(8,128)(2,1)} %collective-permute-done), channel_id=1, source_target_pairs={{0,2},{2,4},{4,6},{6,0},{1,3},{3,5},{5,7},{7,1},{8,10},{10,12},{12... | collective-permute-start | bytes 6291464 | tf_op jit(solution)/shard_map/ppermute | solution.py:19
  167.3 1.2 copy-start.3
  169.8 2.4 copy-start.4
  173.5 1.4 copy-start.6
  173.5 1.5 copy-start.5
  231.3 3.3 copy-start.1
  252.0 3.3 copy-start.1
  272.8 3.3 copy-start.1
  293.5 3.3 copy-start.1
  314.2 3.3 copy-start.1
  335.0 3.3 copy-start.1
  355.7 3.3 copy-start.1
  376.4 3.3 copy-start.1
  401.2 98.2 %all-to-all-start = ((f32[4,256,1024]{2,1,0:T(8,128)}), f32[4,256,1024]{2,1,0:T(8,128)}, u32[]{:S(2)}, u32[]{:S(2)}) async-start(f32[4,256,1024]{2,1,0:T(8,128)} %all_to_all.24), calls=%async_computation.1 | async-start | bytes 8388608 | tf_op jit(solution)/shard_map/all_to_all | solution.py:127
  406.0 303.4 %all-reduce.2.cloned.1.call-start = ((), (), s32[]{:S(2)}) async-start(), calls=%async_computation.8 | async-start | bytes 33554432 | tf_op jit(solution)/shard_map/psum | solution.py:49
  499.3 97.7 %all-to-all-start.1 = ((f32[4,256,1024]{2,1,0:T(8,128)}), f32[4,256,1024]{2,1,0:T(8,128)}, u32[]{:S(2)}, u32[]{:S(2)}) async-start(f32[4,256,1024]{2,1,0:T(8,128)} %all_to_all.27), calls=%async_computation.3 | async-start | bytes 8388608 | tf_op jit(solution)/shard_map/all_to_all | solution.py:128
  504.3 222.6 %reduce-scatter.6.cloned.1.call-start = ((), (), s32[]{:S(2)}) async-start(), calls=%async_computation.6 | async-start | bytes 786432 | tf_op jit(solution)/shard_map/reduce_scatter | solution.py:131
  514.0 214.7 %reduce-scatter.8.cloned.1.call-start = ((), (), s32[]{:S(2)}) async-start(), calls=%async_computation.7 | async-start | bytes 786432 | tf_op jit(solution)/shard_map/reduce_scatter | solution.py:132
Sparse Core Ops, SparseCore 0:
  167.4 53.6 reduce-scatter.3
  514.1 14.7 reduce-scatter.5
  606.6 12.7 reduce-scatter.7
Sparse Core Ops, SparseCore 1:
  420.9 288.5 all-reduce.1
